TPU v7x, 32 devices: a whole 2x2x4 slice. The times are simulated.
32 devices in a mesh: groups: 2 (over x), ctx: 16 (over z, y, core).
Axes of the slice: x: 2, y: 2, z: 4, core: 2. Of those that a mesh axis runs over, the one named last changes fastest.
Arguments:
- keys: bfloat16 [16384, 128], P(('groups', 'ctx')), parts along dimension 0, may hold values from -6 to 6
- queries: bfloat16 [8192, 1024], P(('groups', 'ctx')), parts along dimension 0, may hold values from -240 to 240
- teacher_map: bfloat16 [8192, 512], P(('groups', 'ctx')), parts along dimension 0, may hold values from 0.0099487305 to 1
- slab_index: int32 [32], P(('groups', 'ctx')), parts along dimension 0, may hold values from 0 to 31
- pos_gain: float32 [32, 128], replicated, may hold values from 0.1 to 1.9
- w_comp: bfloat16 [128, 128], replicated, may hold values from -0.09375 to 0.09375
Outputs:
- loss: float32 [2], P('groups'), parts along dimension 0
- grad_queries: bfloat16 [8192, 1024], P(('groups', 'ctx')), parts along dimension 0
- grad_keys: bfloat16 [16384, 128], P(('groups', 'ctx')), parts along dimension 0
- grad_comp: float32 [256, 128], P('groups'), parts along dimension 0
- grad_gain: float32 [64, 128], P('groups'), parts along dimension 0
There are 2 independent parts, one for each index of `groups`. A program takes and returns all parts, laid end to end along the dimension named above; an argument that names none is the same for every part. Nothing has to cross between parts.
All inputs are finite; a program needn't handle non-finite values.
Results may differ from a plain program's by a relative error of at most 0.009.
The roundings to bfloat16 on the way count: a program that leaves them out, or rounds other values in their place, can miss the bound.
Values may be sent and summed in bfloat16 or wider, within the bound.
A program may use at most 64 MiB of HBM per device.

v0:
```python
import jax
import jax.numpy as jnp
from jax import lax
from jax.sharding import PartitionSpec as P

DH = 128
HEADS = 8
KERNEL = 32
STRIDE = 16
KBLK = 512


big_negative = -1e30
loss_scale = 256.0


def shifted_2(array, axis, by):
    size = lax.axis_size(axis)
    pairs = [(i, i + by) for i in range(size) if 0 <= i + by < size]
    return lax.ppermute(array, axis, pairs)


def body(keys, queries, teacher_map, slab_index, pos_gain, w_comp):
    f32 = jnp.float32
    inv = DH ** (-0.5)
    rows = queries.shape[0]
    count = teacher_map.shape[1]
    tiles = count // KBLK
    highest = lax.Precision.HIGHEST
    next_rows = shifted_2(keys[:STRIDE], "ctx", -1)
    lower = keys.reshape(-1, STRIDE, DH).astype(f32)
    upper = jnp.concatenate([keys[STRIDE:], next_rows], axis=0).reshape(-1, STRIDE, DH).astype(f32)
    pooled = (
        jnp.sum(lower * pos_gain[:STRIDE], axis=1) + jnp.sum(upper * pos_gain[STRIDE:], axis=1)
    ).astype(jnp.bfloat16)
    comp_local = jnp.dot(pooled, w_comp, preferred_element_type=f32).astype(jnp.bfloat16)
    comp_all = lax.all_gather(comp_local, "ctx", axis=0, tiled=True)
    places = slab_index[0] * rows + jnp.arange(rows, dtype=jnp.int32)
    head_rows = queries.reshape(rows, HEADS, DH)
    all_cols = jnp.arange(count, dtype=jnp.int32)
    seen_all = (STRIDE * all_cols + KERNEL - 1)[None, :] <= places[:, None]
    teach_total = jnp.sum(jnp.where(seen_all, teacher_map.astype(f32), 0.0), axis=1, keepdims=True)
    safe_total = jnp.where(teach_total > 0, teach_total, 1.0)

    def tile(start, size):
        block = lax.dynamic_slice_in_dim(comp_all, start, size, 0)
        scores = jnp.einsum("thd,jd->htj", head_rows, block, preferred_element_type=f32) * inv
        column = start + jnp.arange(size, dtype=jnp.int32)
        visible = (STRIDE * column + KERNEL - 1)[None, :] <= places[:, None]
        return (block, scores, visible)

    def first_pass(index, carry):
        top, total = carry
        _, scores, visible = tile(index * KBLK, KBLK)
        masked = jnp.where(visible[None], scores, big_negative)
        new_top = jnp.maximum(top, jnp.max(masked, axis=2))
        expo = jnp.where(visible[None], jnp.exp(masked - new_top[..., None]), 0.0)
        return (new_top, total * jnp.exp(top - new_top) + jnp.sum(expo, axis=2))

    top0 = jnp.full((HEADS, rows), big_negative, f32)
    top, total = lax.fori_loop(0, tiles, first_pass, (top0, jnp.zeros((HEADS, rows), f32)))
    lse = jnp.where(total > 0, top + jnp.log(jnp.where(total > 0, total, 1.0)), 0.0)

    def tile_terms(start, size):
        block, scores, visible = tile(start, size)
        shifted = jnp.where(visible[None], scores - lse[..., None], big_negative)
        head_top = jnp.max(shifted, axis=0)
        logm = (
            head_top
            + jnp.log(jnp.sum(jnp.exp(shifted - head_top), axis=0))
            - jnp.log(jnp.float32(HEADS))
        )
        logm = jnp.where(visible, logm, 0.0)
        prob = jnp.where(visible[None], jnp.exp(shifted), 0.0)
        ratio = jnp.where(visible[None], jnp.exp(shifted - logm[None]), 0.0) / HEADS
        teach = lax.dynamic_slice_in_dim(teacher_map, start, size, 1).astype(f32)
        tprob = jnp.where(visible, teach / safe_total, 0.0)
        logt = jnp.where(visible, jnp.log(teach) - jnp.log(safe_total), 0.0)
        return (block, logm, prob, ratio, tprob, logt)

    def second_pass(index, carry):
        kl_sum, cvec = carry
        _, logm, prob, ratio, tprob, logt = tile_terms(index * KBLK, KBLK)
        return (
            kl_sum + jnp.sum(tprob * (logt - logm)),
            cvec + jnp.sum(tprob[None] * ratio, axis=2),
        )

    kl_sum, cvec = lax.fori_loop(
        0, tiles, second_pass, (jnp.zeros((), f32), jnp.zeros((HEADS, rows), f32))
    )

    def grad_tile(start, size):
        block, logm, prob, ratio, tprob, logt = tile_terms(start, size)
        grad = (loss_scale * (prob * cvec[..., None] - tprob[None] * ratio)).astype(jnp.bfloat16)
        return (grad, block)

    def key_term(grad):
        return jnp.einsum("htj,thd->jd", grad, head_rows, preferred_element_type=f32) * inv

    def third_pass(index, carry):
        grad_q, grad_c = carry
        start = index * KBLK
        grad, block = grad_tile(start, KBLK)
        grad_q = grad_q + jnp.einsum("htj,jd->thd", grad, block, preferred_element_type=f32)
        grad_c = lax.dynamic_update_slice_in_dim(grad_c, key_term(grad), start, 0)
        return (grad_q, grad_c)

    start_q = jnp.zeros((rows, HEADS, DH), f32)
    grad_q, grad_c = lax.fori_loop(0, tiles, third_pass, (start_q, jnp.zeros((count, DH), f32)))
    own_grads = lax.psum_scatter(grad_c, "ctx", scatter_dimension=0, tiled=True)
    grad_queries = (grad_q * inv).reshape(rows, HEADS * DH).astype(jnp.bfloat16)
    grad_pooled = jnp.dot(own_grads, w_comp.astype(f32).T, precision=highest)
    comp_part = jnp.dot(pooled.astype(f32).T, own_grads, precision=highest)
    gain_low = jnp.einsum("jd,jpd->pd", grad_pooled, lower, precision=highest)
    gain_high = jnp.einsum("jd,jpd->pd", grad_pooled, upper, precision=highest)
    gain_part = jnp.concatenate([gain_low, gain_high], axis=0)
    grad_comp, grad_gain, kl_total = lax.psum((comp_part, gain_part, kl_sum), "ctx")
    loss = (kl_total / (rows * lax.axis_size("ctx"))).reshape(1)
    low_part = (grad_pooled[:, None, :] * pos_gain[:STRIDE]).reshape(-1, DH)
    high_part = (grad_pooled[:, None, :] * pos_gain[STRIDE:]).reshape(-1, DH)
    carried = shifted_2(high_part[-STRIDE:], "ctx", 1)
    grad_keys = (low_part + jnp.concatenate([carried, high_part[:-STRIDE]], axis=0)).astype(
        jnp.bfloat16
    )
    return (loss, grad_queries, grad_keys, grad_comp, grad_gain)


def solution(mesh):
    in_specs = (
        P(("groups", "ctx"), None),
        P(("groups", "ctx"), None),
        P(("groups", "ctx"), None),
        P(("groups", "ctx")),
        P(),
        P(),
    )
    out_specs = (
        P("groups"),
        P(("groups", "ctx"), None),
        P(("groups", "ctx"), None),
        P("groups", None),
        P("groups", None),
    )
    return jax.shard_map(body, mesh=mesh, in_specs=in_specs, out_specs=out_specs, check_vma=False)
```

profile of v0, /device:TPU:0, one launch (start us, length us, event | category | flops | bytes accessed | tf_op | source)
XLA Modules:
  0.0 203.2 jit_solution(1756288123377649201)
XLA Ops:
  7.2 0.0 copy-start
  7.2 0.0 reduce-scatter.2.cloned.1.call-start
  7.2 0.7 slice.28
  8.0 1.3 collective-permute-start
  9.3 1.1 copy.19
  11.0 0.1 broadcast_compare_fusion
  11.2 0.1 fusion.36
  11.3 0.7 fusion.64
  12.1 1.0 multiply_reduce_fusion.3
  13.0 0.9 slice.27
  13.9 0.0 collective-permute-done
  13.9 0.1 multiply_reduce_fusion.2
  14.0 0.9 convolution_convert_fusion
  14.9 24.1 %all_gather.3 = bf16[512,128]{1,0:T(8,128)(2,1)S(1)} all-gather(bf16[32,128]{1,0:T(8,128)(2,1)S(1)} %convolution_convert_fusion), channel_id=1, replica_groups=mesh['groups'=2,'ctx'=16] {'ctx'}, dimensions={0}, use_global_device_ids=true | all-gather | bytes 139264 | tf_op jit(solution)/shard_map/all_gather | solution.py:37
  39.0 0.0 copy-done
  39.0 0.8 fusion.2
  39.8 0.0 copy-start.1
  39.8 1.0 select_reduce_fusion
  40.9 0.7 fusion.32
  41.5 0.2 copy-done.1
  41.7 1.0 exponential_reduce_fusion
  42.8 1.0 fusion.35
  43.7 7.8 %fusion.27 = f32[512,128]{1,0:T(8,128)} fusion(f32[256,512]{0,1:T(8,128)S(1)} %get-tuple-element.96, f32[256,512]{0,1:T(8,128)S(1)} %get-tuple-element.93, pred[256,512]{0,1:T(8,128)(4,1)S(1)} %broadcast_compare_fusion, f32[512,256,8]{1,0,2:T(8,128)} %copy-done.1, f32[8,256]{1,0:T(8,128)S(1)} %compare_select_fusion.3, bf16[256,1024]{1,0:T(8,128)(2,1)S(1)} %copy-done), kind=kOutput, calls=%fused_computation.25 | convolution fusion | flops 286329344 | bytes 6168576 | tf_op jit(solution)/shard_map/while/body/eval_jaxpr/htj,thd->jd/dot_general | solution.py:99
  51.6 0.0 reduce-scatter.2.cloned.1.call-update
  51.6 0.0 copy-start.3
  51.6 0.0 copy-start.2
  51.6 0.2 all-reduce.3.cloned.1.call-start
  51.9 7.3 %fusion.25 = bf16[128,8,256]{2,0,1:T(8,128)(2,1)S(1)} fusion(f32[256,512]{0,1:T(8,128)S(1)} %get-tuple-element.96, f32[256,512]{0,1:T(8,128)S(1)} %get-tuple-element.93, pred[256,512]{0,1:T(8,128)(4,1)S(1)} %broadcast_compare_fusion, f32[512,256,8]{1,0,2:T(8,128)} %copy-done.1, f32[8,256]{1,0:T(8,128)S(1)} %compare_select_fusion.3, ...), kind=kOutput, calls=%fused_computation.23 | convolution fusion | flops 286788096 | bytes 6037504 | tf_op jit(solution)/shard_map/while/body/eval_jaxpr/htj,jd->thd/dot_general | solution.py:105
  59.2 1.0 copy.23
  60.2 44.2 %reduce-scatter.2.cloned.1.call-done = f32[32,128]{1,0:T(8,128)} async-done(((f32[512,128]{1,0:T(8,128)}), f32[32,128]{1,0:T(8,128)}) %reduce-scatter.2.cloned.1.call-update) | async-done | bytes 16400 | tf_op jit(solution)/shard_map/reduce_scatter | solution.py:111
  104.4 0.0 copy-done.3
  104.4 0.8 fusion.65
  105.2 0.1 broadcast_multiply_fusion.1
  105.3 1.3 collective-permute-start.1
  106.6 1.6 fusion.66
  108.2 0.0 all-reduce.3.cloned.1.call-update
  108.2 0.0 copy-done.2
  108.3 0.1 multiply_reduce_fusion.1
  108.3 59.7 %all-reduce = (f32[]{:T(128)}, f32[32,128]{1,0:T(8,128)}) all-reduce(f32[]{:T(128)} %get-tuple-element.92, f32[32,128]{1,0:T(8,128)S(1)} %pad_maximum_fusion.1), channel_id=1, replica_groups=mesh['groups'=2,'ctx'=16] {'ctx'}, use_global_device_ids=true, to_apply=%region_8.9 | all-reduce | flops 4097 | bytes 32776 | tf_op jit(solution)/shard_map/psum | solution.py:118
  168.7 0.0 collective-permute-done.1
  168.7 0.7 fusion.44
  169.4 24.4 %all-reduce.3.cloned.1.call-done = f32[128,128]{1,0:T(8,128)} async-done(((f32[128,128]{1,0:T(8,128)}), f32[128,128]{1,0:T(8,128)}) %all-reduce.3.cloned.1.call-update) | async-done | bytes 65552 | tf_op jit(solution)/shard_map/psum | solution.py:118
  193.7 1.5 copy.51
  (9 shorter events, 0.1 us)
Async XLA Ops:
  7.2 31.8 %copy-start = (bf16[256,1024]{1,0:T(8,128)(2,1)S(1)}, bf16[256,1024]{1,0:T(8,128)(2,1)}, u32[]{:S(2)}) copy-start(bf16[256,1024]{1,0:T(8,128)(2,1)} %param.7) | copy-start | bytes 1572868
  7.2 97.2 %reduce-scatter.2.cloned.1.call-start = ((), (), s32[]{:S(2)}) async-start(), calls=%async_computation.1 | async-start | bytes 278528 | tf_op jit(solution)/shard_map/reduce_scatter | solution.py:111
  8.0 6.0 %collective-permute-start = (bf16[16,128]{1,0:T(8,128)(2,1)S(1)}, bf16[16,128]{1,0:T(8,128)(2,1)S(1)}, u32[]{:S(2)}, u32[]{:S(2)}) collective-permute-start(bf16[16,128]{1,0:T(8,128)(2,1)S(1)} %slice.28), channel_id=1, source_target_pairs={{1,0},{2,1},{3,2},{4,3},{5,4},{6,5},{7,6},{8,7},{9,8},{10,9},{11,1... | collective-permute-start | bytes 12296 | tf_op jit(solution)/shard_map/ppermute | solution.py:20
  39.8 1.9 copy-start.1
  51.6 52.8 %copy-start.3 = (bf16[128,128]{1,0:T(8,128)(2,1)S(1)}, bf16[128,128]{1,0:T(8,128)(2,1)}, u32[]{:S(2)}) copy-start(bf16[128,128]{1,0:T(8,128)(2,1)} %param.11) | copy-start | bytes 98308
  51.6 56.6 %copy-start.2 = (bf16[512,128]{1,0:T(8,128)(2,1)S(1)}, bf16[512,128]{1,0:T(8,128)(2,1)}, u32[]{:S(2)}) copy-start(bf16[512,128]{1,0:T(8,128)(2,1)} %param.6) | copy-start | bytes 393220
  51.6 142.1 %all-reduce.3.cloned.1.call-start = ((), (), s32[]{:S(2)}) async-start(), calls=%async_computation.2 | async-start | bytes 131072 | tf_op jit(solution)/shard_map/psum | solution.py:118
  105.3 63.3 %collective-permute-start.1 = (f32[16,128]{1,0:T(8,128)S(1)}, f32[16,128]{1,0:T(8,128)S(1)}, u32[]{:S(2)}, u32[]{:S(2)}) collective-permute-start(f32[16,128]{1,0:T(8,128)S(1)} %slice_bitcast_fusion), channel_id=1, source_target_pairs={{0,1},{1,2},{2,3},{3,4},{4,5},{5,6},{6,7},{7,8},{8,9},{9,10},{10,1... | collective-permute-start | bytes 24584 | tf_op jit(solution)/shard_map/ppermute | solution.py:20
Sparse Core Ops, SparseCore 0:
  51.7 52.5 reduce-scatter.1
  108.4 85.3 all-reduce.2
where the time goes:
time: 205 us; the launch traced here: 203 us
  blocking collectives  83.7 us (41%)
  waiting for transfers between devices  68.6 us (33%)
  matrix products  19.2 us (9%)
  between operations  16.7 us (8%)
  local copies, waits for them, and re-layouts  6.18 us (3%)
  other arithmetic  5.92 us (3%)
  starting transfers between devices  2.83 us (1%)
    psum x1, blocking collectives, body(): lax.psum((comp_part, gain_part, kl_sum), 'ctx')  59.7 us
    reduce_scatter x1, waiting for transfers between devices, body(): own_grads = lax.psum_scatter(grad_c, 'ctx', scatter_dimension=0, tiled=True)  44.2 us
    psum x1, waiting for transfers between devices, body(): lax.psum((comp_part, gain_part, kl_sum), 'ctx')  24.4 us
    all_gather x1, blocking collectives, body(): comp_all = lax.all_gather(comp_local, 'ctx', axis=0, tiled=True)  24.1 us
    dot_general x1, matrix products, key_term(): jnp.einsum('htj,thd->jd', grad, head_rows, preferred_element_type=f32) * inv  7.83 us
    dot_general x1, matrix products, third_pass(): jnp.einsum('htj,jd->thd', grad, block, preferred_element_type=f32)  7.3 us
  transfers between devices with their start and end apart: 4, of which 2 were waited for; matrix products, arithmetic and copies ran while one was open for 7% of the time, Pallas kernels for 0%

commit v1 on v0

v1 whole, which is shorter than its diff:
```python
import functools

import jax
import jax.numpy as jnp
from jax import lax
from jax.experimental import pallas as pl
from jax.experimental.pallas import tpu as pltpu
from jax.sharding import PartitionSpec as P

DH = 128
HEADS = 8
KERNEL = 32
STRIDE = 16
CHUNK = 512

big_negative = -1e30
loss_scale = 256.0
f32 = jnp.float32
bf16 = jnp.bfloat16


def split3(x):
    first = x.astype(bf16)
    rest = x - first.astype(f32)
    second = rest.astype(bf16)
    third = (rest - second.astype(f32)).astype(bf16)
    return first, second, third


def remote(src, dst, send_sem, recv_sem, device):
    return pltpu.make_async_remote_copy(
        src_ref=src,
        dst_ref=dst,
        send_sem=send_sem,
        recv_sem=recv_sem,
        device_id={"ctx": device},
        device_id_type=pl.DeviceIdType.MESH,
    )


def kernel(
    n, rb, tr, rc, rg,
    slab_ref, keys_ref, gain_ref, w_ref, q_hbm, t_hbm,
    loss_ref, gq_hbm, gk_ref, gcomp_ref, ggain_ref,
    q_v, t_v, gq_v, pool_v, part_v, halo_v, pooled_v, comp_v, s_v, g_v, p_v, rs_v,
    a_out, a_in, b_out, b_in, gp_v, carry_v,
    local_sem, pool_s, pool_r, part_s, part_r, rs_s, rs_r, a_s, a_r, b_s, b_r, side_sem,
):
    me = lax.axis_index("ctx")
    rows, count = t_v.shape
    nb = count // n
    inv = DH ** (-0.5)

    q_copy = pltpu.make_async_copy(q_hbm, q_v, local_sem.at[0])
    t_copy = pltpu.make_async_copy(t_hbm, t_v, local_sem.at[1])
    q_copy.start()
    t_copy.start()

    barrier = pltpu.get_barrier_semaphore()

    def greet(k, _):
        pl.semaphore_signal(
            barrier, inc=1, device_id={"ctx": lax.rem(me + k, n)},
            device_id_type=pl.DeviceIdType.MESH,
        )
        return 0

    lax.fori_loop(1, n, greet, 0)

    keys3 = keys_ref[...].astype(f32).reshape(nb, STRIDE, DH)
    gain_lo = gain_ref[0:STRIDE, :]
    gain_hi = gain_ref[STRIDE:KERNEL, :]
    low = jnp.sum(keys3 * gain_lo[None], axis=1)
    high = jnp.sum(keys3 * gain_hi[None], axis=1)
    pool_v[me] = (low + jnp.concatenate([high[1:], high[:1]], axis=0)).astype(bf16)
    part_v[me] = jnp.concatenate(
        [jnp.broadcast_to(low[nb - 1 : nb], (8, DH)), jnp.broadcast_to(high[0:1], (8, DH))], axis=0
    )
    part_v[n] = jnp.zeros((16, DH), f32)

    @pl.when(me == n - 1)
    def _():
        halo_v[...] = jnp.zeros((STRIDE, DH), bf16)

    @pl.when(me == 0)
    def _():
        carry_v[...] = jnp.zeros((8, DH), f32)

    pl.semaphore_wait(barrier, n - 1)

    def pool_copy(dst, slot):
        return remote(pool_v.at[slot], pool_v.at[slot], pool_s.at[dst], pool_r.at[slot], dst)

    def part_copy(dst, slot):
        return remote(part_v.at[slot], part_v.at[slot], part_s.at[dst], part_r.at[slot], dst)

    def send_pool(k, _):
        dst = lax.rem(me + k, n)
        pool_copy(dst, me).start()
        part_copy(dst, me).start()
        return 0

    lax.fori_loop(1, n, send_pool, 0)

    def halo_copy(dst):
        return remote(
            keys_ref.at[pl.ds(0, STRIDE)], halo_v, side_sem.at[0], side_sem.at[1], dst
        )

    @pl.when(me > 0)
    def _():
        halo_copy(me - 1).start()

    def take_pool(k, _):
        src = lax.rem(me + k, n)
        pool_copy(src, src).wait_recv()
        part_copy(src, src).wait_recv()
        return 0

    lax.fori_loop(1, n, take_pool, 0)
    last_row = lax.broadcasted_iota(jnp.int32, (nb, DH), 0) == nb - 1

    def place_pool(d, _):
        edge = part_v[d][0:1] + part_v[d + 1][8:9]
        block = jnp.where(last_row, edge, pool_v[d].astype(f32)).astype(bf16)
        at = pl.multiple_of(d * nb, nb)
        pooled_v[pl.ds(at, nb), :] = block
        comp_v[pl.ds(at, nb), :] = jnp.dot(
            block, w_ref[...], preferred_element_type=f32
        ).astype(bf16)
        return 0

    lax.fori_loop(0, n, place_pool, 0)
    q_copy.wait()
    t_copy.wait()

    place0 = slab_ref[0] * rows
    column_end = STRIDE * lax.broadcasted_iota(jnp.int32, (tr, count), 1) + (KERNEL - 1)
    row_in = lax.broadcasted_iota(jnp.int32, (tr, count), 0)
    nt = (((1,), (1,)), ((), ()))
    tn = (((0,), (0,)), ((), ()))

    def group(base, first, kl):
        rows_at = pl.ds(base, rb)
        for h in range(HEADS):
            qh = q_v[rows_at, h * DH : (h + 1) * DH]
            for c0 in range(0, count, CHUNK):
                s_v[h, :, c0 : c0 + CHUNK] = (
                    lax.dot_general(
                        qh, comp_v[c0 : c0 + CHUNK, :], nt, preferred_element_type=f32
                    )
                    * inv
                )

        def tile(i, kl):
            off = pl.multiple_of(i * tr, tr)
            here = pl.ds(off, tr)
            visible = column_end <= place0 + base + off + row_in
            top_all = jnp.full((tr, count), 2 * big_negative, f32)
            for h in range(HEADS):
                s = jnp.where(visible, s_v[h, here, :], big_negative)
                top = jnp.max(s, axis=1, keepdims=True)
                total = jnp.sum(jnp.exp(s - top), axis=1, keepdims=True)
                lse = jnp.where(top > 0.5 * big_negative, top + jnp.log(total), 0.0)
                x = s - lse
                s_v[h, here, :] = x
                top_all = jnp.maximum(top_all, x)
            mass = jnp.zeros((tr, count), f32)
            for h in range(HEADS):
                u = jnp.exp(s_v[h, here, :] - top_all)
                s_v[h, here, :] = u
                mass = mass + u
            teach = t_v[pl.ds(pl.multiple_of(base + off, tr), tr), :].astype(f32)
            seen = jnp.where(visible, teach, 0.0)
            teach_total = jnp.sum(seen, axis=1, keepdims=True)
            safe = jnp.where(teach_total > 0, teach_total, 1.0)
            tprob = seen / safe
            logm = jnp.where(visible, top_all + jnp.log(mass) - jnp.log(f32(HEADS)), 0.0)
            kl = kl + jnp.sum(
                tprob * (jnp.log(teach) - jnp.log(safe) - logm), axis=1, keepdims=True
            )
            weight = tprob / mass
            peak = jnp.exp(top_all)
            weight_s = loss_scale * weight
            for h in range(HEADS):
                u = s_v[h, here, :]
                cvec = loss_scale * jnp.sum(u * weight, axis=1, keepdims=True)
                g_v[h, here, :] = (u * (peak * cvec - weight_s)).astype(bf16)
            return kl

        kl = lax.fori_loop(0, rb // tr, tile, kl)
        for c0 in range(0, count, CHUNK):
            acc = jnp.zeros((DH, CHUNK), f32)
            for h in range(HEADS):
                acc = acc + lax.dot_general(
                    q_v[rows_at, h * DH : (h + 1) * DH], g_v[h, :, c0 : c0 + CHUNK], tn,
                    preferred_element_type=f32,
                )
            add = acc.T * inv
            if first is None:
                p_v[c0 : c0 + CHUNK, :] = add
            else:
                p_v[c0 : c0 + CHUNK, :] = p_v[c0 : c0 + CHUNK, :] + add
        return kl

    def query_grads(base):
        for h in range(HEADS):
            gq_v[pl.ds(base, rb), h * DH : (h + 1) * DH] = (
                jnp.dot(g_v[h], comp_v[...], preferred_element_type=f32) * inv
            ).astype(bf16)

    kl0 = jnp.zeros((tr, 1), f32)
    if rb == rows:
        kl = group(0, None, kl0)
    else:
        p_v[...] = jnp.zeros_like(p_v)

        def step(i, kl):
            base = pl.multiple_of(i * rb, rb)
            kl = group(base, False, kl)
            query_grads(base)
            return kl

        kl = lax.fori_loop(0, rows // rb, step, kl0)

    def rs_copy(dst, slot):
        at = pl.multiple_of(dst * nb, nb)
        return remote(p_v.at[pl.ds(at, nb)], rs_v.at[slot], rs_s.at[dst], rs_r.at[slot], dst)

    def send_rs(k, _):
        rs_copy(lax.rem(me + k, n), me).start()
        return 0

    lax.fori_loop(1, n, send_rs, 0)
    rs_v[me] = p_v[pl.ds(pl.multiple_of(me * nb, nb), nb), :]

    if rb == rows:
        query_grads(0)
    gq_copy = pltpu.make_async_copy(gq_v, gq_hbm, local_sem.at[2])
    gq_copy.start()

    @pl.when(me < n - 1)
    def _():
        halo_copy(me).wait_recv()

    upper3 = jnp.concatenate(
        [keys3[1:], halo_v[...].astype(f32).reshape(1, STRIDE, DH)], axis=0
    )

    def take_rs(k, _):
        rs_copy(lax.rem(me + k, n), lax.rem(me + k, n)).wait_recv()
        return 0

    lax.fori_loop(1, n, take_rs, 0)
    own = lax.fori_loop(1, n, lambda d, total: total + rs_v[d], rs_v[0])

    own3 = split3(own)
    gp3 = lax.dot_general(
        jnp.concatenate(own3, axis=0), w_ref[...], nt, preferred_element_type=f32
    )
    grad_pooled = (gp3[2 * nb :] + gp3[nb : 2 * nb]) + gp3[:nb]
    gp_v[...] = grad_pooled

    def carry_copy(dst):
        return remote(
            gp_v.at[pl.ds(nb - 8, 8)], carry_v, side_sem.at[2], side_sem.at[3], dst
        )

    @pl.when(me < n - 1)
    def _():
        carry_copy(me + 1).start()

    pooled_own = pooled_v[pl.ds(pl.multiple_of(me * nb, nb), nb), :]
    comp_part = lax.dot_general(
        jnp.concatenate([pooled_own] * 3, axis=0),
        jnp.concatenate(own3[::-1], axis=0),
        tn,
        preferred_element_type=f32,
    )
    gain_part = jnp.concatenate(
        [
            jnp.sum(grad_pooled[:, None, :] * keys3, axis=0),
            jnp.sum(grad_pooled[:, None, :] * upper3, axis=0),
        ],
        axis=0,
    )
    kl_row = jnp.broadcast_to(jnp.sum(kl, axis=0, keepdims=True), (1, DH))
    slot_rows = a_out.shape[1]
    for d in range(n):
        pieces = [comp_part[d * rc : (d + 1) * rc]]
        if (d + 1) * rg <= KERNEL:
            pieces.append(gain_part[d * rg : (d + 1) * rg])
        else:
            pieces.append(jnp.zeros((rg, DH), f32))
        pieces.append(jnp.broadcast_to(kl_row, (slot_rows - rc - rg, DH)))
        a_out[d] = jnp.concatenate(pieces, axis=0)

    def a_copy(dst, slot):
        return remote(a_out.at[dst], a_in.at[slot], a_s.at[dst], a_r.at[slot], dst)

    def send_a(k, _):
        a_copy(lax.rem(me + k, n), me).start()
        return 0

    lax.fori_loop(1, n, send_a, 0)
    a_in[me] = a_out[me]

    @pl.when(me > 0)
    def _():
        carry_copy(me).wait_recv()

    def take_a(k, _):
        a_copy(lax.rem(me + k, n), lax.rem(me + k, n)).wait_recv()
        return 0

    lax.fori_loop(1, n, take_a, 0)
    b_out[...] = lax.fori_loop(1, n, lambda d, total: total + a_in[d], a_in[0])

    def b_copy(dst, slot):
        return remote(b_out, b_in.at[slot], b_s.at[dst], b_r.at[slot], dst)

    def send_b(k, _):
        b_copy(lax.rem(me + k, n), me).start()
        return 0

    lax.fori_loop(1, n, send_b, 0)
    b_in[me] = b_out[...]
    loss_ref[...] = b_out[rc + rg : rc + rg + 1, :] * (1.0 / (rows * n))

    before = jnp.concatenate([carry_v[7:8, :], grad_pooled[: nb - 1]], axis=0)
    grad_keys = grad_pooled[:, None, :] * gain_lo[None] + before[:, None, :] * gain_hi[None]
    gk_ref[...] = grad_keys.reshape(nb * STRIDE, DH).astype(bf16)

    def drop_sends(k, _):
        dst = lax.rem(me + k, n)
        pool_copy(dst, me).wait_send()
        part_copy(dst, me).wait_send()
        rs_copy(dst, me).wait_send()
        a_copy(dst, me).wait_send()
        return 0

    lax.fori_loop(1, n, drop_sends, 0)

    @pl.when(me > 0)
    def _():
        halo_copy(me - 1).wait_send()

    @pl.when(me < n - 1)
    def _():
        carry_copy(me + 1).wait_send()

    def take_b(k, _):
        other = lax.rem(me + k, n)
        b_copy(other, other).wait_recv()
        b_copy(other, me).wait_send()
        return 0

    lax.fori_loop(1, n, take_b, 0)
    for d in range(n):
        gcomp_ref[d * rc : (d + 1) * rc, :] = b_in[d, 0:rc, :]
        if (d + 1) * rg <= KERNEL:
            ggain_ref[d * rg : (d + 1) * rg, :] = b_in[d, rc : rc + rg, :]
    gq_copy.wait()


def body(n, keys, queries, teacher_map, slab_index, pos_gain, w_comp):
    rows, count = teacher_map.shape
    nb = count // n
    rb = rows if count <= 1024 else 32
    tr = min(rb, 32 if count <= 1024 else 16)
    rc = -(-DH // n)
    rg = -(-KERNEL // n)
    slot_rows = -(-(rc + rg + 1) // 8) * 8
    dma = pltpu.SemaphoreType.DMA
    vmem = pl.BlockSpec(memory_space=pltpu.VMEM)
    hbm = pl.BlockSpec(memory_space=pl.ANY)
    loss, gq, gk, gcomp, ggain = pl.pallas_call(
        functools.partial(kernel, n, rb, tr, rc, rg),
        out_shape=(
            jax.ShapeDtypeStruct((1, DH), f32),
            jax.ShapeDtypeStruct((rows, HEADS * DH), bf16),
            jax.ShapeDtypeStruct(keys.shape, bf16),
            jax.ShapeDtypeStruct((DH, DH), f32),
            jax.ShapeDtypeStruct((KERNEL, DH), f32),
        ),
        in_specs=[pl.BlockSpec(memory_space=pltpu.SMEM), vmem, vmem, vmem, hbm, hbm],
        out_specs=(vmem, hbm, vmem, vmem, vmem),
        scratch_shapes=[
            pltpu.VMEM((rows, HEADS * DH), bf16),
            pltpu.VMEM((rows, count), bf16),
            pltpu.VMEM((rows, HEADS * DH), bf16),
            pltpu.VMEM((n, nb, DH), bf16),
            pltpu.VMEM((n + 1, 16, DH), f32),
            pltpu.VMEM((STRIDE, DH), bf16),
            pltpu.VMEM((count, DH), bf16),
            pltpu.VMEM((count, DH), bf16),
            pltpu.VMEM((HEADS, rb, count), f32),
            pltpu.VMEM((HEADS, rb, count), bf16),
            pltpu.VMEM((count, DH), f32),
            pltpu.VMEM((n, nb, DH), f32),
            pltpu.VMEM((n, slot_rows, DH), f32),
            pltpu.VMEM((n, slot_rows, DH), f32),
            pltpu.VMEM((slot_rows, DH), f32),
            pltpu.VMEM((n, slot_rows, DH), f32),
            pltpu.VMEM((nb, DH), f32),
            pltpu.VMEM((8, DH), f32),
            dma((3,)),
        ]
        + [dma((n,))] * 10
        + [dma((4,))],
        compiler_params=pltpu.CompilerParams(
            collective_id=0, has_side_effects=True, vmem_limit_bytes=48 * 1024 * 1024
        ),
    )(slab_index, keys, pos_gain, w_comp, queries, teacher_map)
    return (loss[0, 0:1], gq, gk, gcomp, ggain)


def solution(mesh):
    in_specs = (
        P(("groups", "ctx"), None),
        P(("groups", "ctx"), None),
        P(("groups", "ctx"), None),
        P(("groups", "ctx")),
        P(),
        P(),
    )
    out_specs = (
        P("groups"),
        P(("groups", "ctx"), None),
        P(("groups", "ctx"), None),
        P("groups", None),
        P("groups", None),
    )
    return jax.shard_map(
        functools.partial(body, mesh.shape["ctx"]),
        mesh=mesh, in_specs=in_specs, out_specs=out_specs, check_vma=False,
    )
```

time: 205 us -> 49.1 us (0.24)
  blocking collectives: 83.7 us -> 0 us
  waiting for transfers between devices: 68.6 us -> 0 us
  Pallas kernels: 0 us -> 39.2 us
  matrix products: 19.2 us -> 0 us
  between operations: 16.7 us -> 2.46 us
  other arithmetic: 5.92 us -> 0 us
  starting transfers between devices: 2.83 us -> 0 us
    psum x1 -> x0, blocking collectives: 59.7 us -> none  [body(): lax.psum((comp_part, gain_part, kl_sum), 'ctx')]
    reduce_scatter x1 -> x0, waiting for transfers between devices: 44.2 us -> none  [body(): own_grads = lax.psum_scatter(grad_c, 'ctx', scatter_dimension=0, tiled=True)]
    pallas_call x0 -> x1, Pallas kernels: none -> 39.2 us  [body(): pl.pallas_call(functools.partial(kernel, n, rb, tr, rc, rg), out_shape=(j...]
    psum x1 -> x0, waiting for transfers between devices: 24.4 us -> none  [body(): lax.psum((comp_part, gain_part, kl_sum), 'ctx')]
    all_gather x1 -> x0, blocking collectives: 24.1 us -> none  [body(): comp_all = lax.all_gather(comp_local, 'ctx', axis=0, tiled=True)]
    dot_general x6 -> x0, matrix products: 19.2 us -> none  [the longest x1 7.83 us: key_term(): jnp.einsum('htj,thd->jd', grad, head_rows, preferred_element_type=f32) * inv]
    reduce_sum x6 -> x0, other arithmetic: 4.23 us -> none  [the longest x1 1.05 us: tile_terms(): jnp.sum(jnp.exp(shifted - head_top), axis=0)]
    unnamed x11 -> x14, local copies, waits for them, and re-layouts: 3.78 us -> 7.05 us
  transfers between devices with their start and end apart: 4 -> 0, of which waited for: 2 -> 0; matrix products, arithmetic and copies ran while one was open for 7% -> 0% of each run, Pallas kernels for 0% -> 0%
where the time goes in v1:
time: 49.1 us; the launch traced here: 48.7 us
  Pallas kernels  39.2 us (80%)
  local copies, waits for them, and re-layouts  7.05 us (14%)
  between operations  2.46 us (5%)
    pallas_call x1, Pallas kernels, body(): pl.pallas_call(functools.partial(kernel, n, rb, tr, rc, rg), out_shape=(j...  39.2 us
    unnamed x14, local copies, waits for them, and re-layouts  7.05 us

profile of v1, /device:TPU:0, one launch (start us, length us, event | category | flops | bytes accessed | tf_op | source)
XLA Modules:
  0.0 48.7 jit_solution(15991726903524789472)
XLA Ops:
  1.3 0.0 copy-start
  1.3 1.0 %copy-done = bf16[256,1024]{1,0:T(8,128)(2,1)S(1)} copy-done((bf16[256,1024]{1,0:T(8,128)(2,1)S(1)}, bf16[256,1024]{1,0:T(8,128)(2,1)}, u32[]{:S(2)}) %copy-start) | copy-done | bytes 524312
  2.3 0.0 copy-start.1
  2.3 0.9 %copy-done.1 = bf16[256,512]{1,0:T(8,128)(2,1)S(1)} copy-done((bf16[256,512]{1,0:T(8,128)(2,1)S(1)}, bf16[256,512]{1,0:T(8,128)(2,1)}, u32[]{:S(2)}) %copy-start.1) | copy-done | bytes 262168
  3.3 0.0 copy-start.2
  3.3 0.9 %copy-done.2 = bf16[512,128]{1,0:T(8,128)(2,1)S(1)} copy-done((bf16[512,128]{1,0:T(8,128)(2,1)S(1)}, bf16[512,128]{1,0:T(8,128)(2,1)}, u32[]{:S(2)}) %copy-start.2) | copy-done | bytes 131096
  4.2 0.0 copy-start.3
  4.2 0.8 %copy-done.3 = bf16[128,128]{1,0:T(8,128)(2,1)S(1)} copy-done((bf16[128,128]{1,0:T(8,128)(2,1)S(1)}, bf16[128,128]{1,0:T(8,128)(2,1)}, u32[]{:S(2)}) %copy-start.3) | copy-done | bytes 32792
  4.9 0.0 copy-start.4
  4.9 0.7 %copy-done.4 = f32[32,128]{1,0:T(8,128)S(1)} copy-done((f32[32,128]{1,0:T(8,128)S(1)}, f32[32,128]{1,0:T(8,128)}, u32[]{:S(2)}) %copy-start.4) | copy-done | bytes 16408
  5.7 39.2 %shard_map.101 = (f32[1,128]{1,0:T(1,128)S(1)}, bf16[256,1024]{1,0:T(8,128)(2,1)S(1)}, bf16[512,128]{1,0:T(8,128)(2,1)S(1)}, f32[128,128]{1,0:T(8,128)S(1)}, f32[32,128]{1,0:T(8,128)S(1)}) custom-call(s32[1]{0:T(128)S(6)} %copy.16.slab_ref, bf16[512,128]{1,0:T(8,128)(2,1)S(1)} %copy-done.2, f32[32,128]{1,0:T(8,128)S(1)} %copy-done.4, ...), custom_call_target="tpu_custom_call" | custom-call | tf_op jit(solution)/shard_map/pallas_call | solution.py:377
  44.9 0.8 %copy.18 = bf16[256,1024]{1,0:T(8,128)(2,1)} copy(bf16[256,1024]{1,0:T(8,128)(2,1)S(1)} %get-tuple-element.21) | data formatting | bytes 1048576
  45.7 0.7 %copy.19 = bf16[512,128]{1,0:T(8,128)(2,1)} copy(bf16[512,128]{1,0:T(8,128)(2,1)S(1)} %get-tuple-element.22) | data formatting | bytes 262144
  46.4 0.6 %copy.20 = f32[128,128]{1,0:T(8,128)} copy(f32[128,128]{1,0:T(8,128)S(1)} %get-tuple-element.23) | data formatting | bytes 131072
  47.0 0.6 %copy.21 = f32[32,128]{1,0:T(8,128)} copy(f32[32,128]{1,0:T(8,128)S(1)} %get-tuple-element.24) | data formatting | bytes 32768
Async XLA Ops:
  1.3 1.0 %copy-start = (bf16[256,1024]{1,0:T(8,128)(2,1)S(1)}, bf16[256,1024]{1,0:T(8,128)(2,1)}, u32[]{:S(2)}) copy-start(bf16[256,1024]{1,0:T(8,128)(2,1)} %q_hbm.1) | copy-start | bytes 1572868
  2.3 0.9 %copy-start.1 = (bf16[256,512]{1,0:T(8,128)(2,1)S(1)}, bf16[256,512]{1,0:T(8,128)(2,1)}, u32[]{:S(2)}) copy-start(bf16[256,512]{1,0:T(8,128)(2,1)} %t_hbm.1) | copy-start | bytes 786436
  3.3 0.9 %copy-start.2 = (bf16[512,128]{1,0:T(8,128)(2,1)S(1)}, bf16[512,128]{1,0:T(8,128)(2,1)}, u32[]{:S(2)}) copy-start(bf16[512,128]{1,0:T(8,128)(2,1)} %keys_ref.1) | copy-start | bytes 393220
  4.2 0.8 %copy-start.3 = (bf16[128,128]{1,0:T(8,128)(2,1)S(1)}, bf16[128,128]{1,0:T(8,128)(2,1)}, u32[]{:S(2)}) copy-start(bf16[128,128]{1,0:T(8,128)(2,1)} %w_ref.1) | copy-start | bytes 98308
  4.9 0.7 %copy-start.4 = (f32[32,128]{1,0:T(8,128)S(1)}, f32[32,128]{1,0:T(8,128)}, u32[]{:S(2)}) copy-start(f32[32,128]{1,0:T(8,128)} %gain_ref.1) | copy-start | bytes 49156

commit v2 on v1

--- a/solution.py
+++ b/solution.py
@@ -40,9 +40,9 @@
 
 def kernel(
     n, rb, tr, rc, rg,
-    slab_ref, keys_ref, gain_ref, w_ref, q_hbm, t_hbm,
+    slab_ref, keys_hbm, gain_hbm, w_hbm, q_hbm, t_hbm,
     loss_ref, gq_hbm, gk_ref, gcomp_ref, ggain_ref,
-    q_v, t_v, gq_v, pool_v, part_v, halo_v, pooled_v, comp_v, s_v, g_v, p_v, rs_v,
+    keys_ref, gain_ref, w_ref, q_v, t_v, gq_v, pool_v, part_v, halo_v, pooled_v, comp_v, s_v, g_v, p_v, rs_v,
     a_out, a_in, b_out, b_in, gp_v, carry_v,
     local_sem, pool_s, pool_r, part_s, part_r, rs_s, rs_r, a_s, a_r, b_s, b_r, side_sem,
 ):
@@ -53,6 +53,12 @@
 
     q_copy = pltpu.make_async_copy(q_hbm, q_v, local_sem.at[0])
     t_copy = pltpu.make_async_copy(t_hbm, t_v, local_sem.at[1])
+    keys_copy = pltpu.make_async_copy(keys_hbm, keys_ref, local_sem.at[3])
+    gain_copy = pltpu.make_async_copy(gain_hbm, gain_ref, local_sem.at[4])
+    w_copy = pltpu.make_async_copy(w_hbm, w_ref, local_sem.at[5])
+    keys_copy.start()
+    gain_copy.start()
+    w_copy.start()
     q_copy.start()
     t_copy.start()
 
@@ -67,16 +73,17 @@
 
     lax.fori_loop(1, n, greet, 0)
 
+    keys_copy.wait()
+    gain_copy.wait()
     keys3 = keys_ref[...].astype(f32).reshape(nb, STRIDE, DH)
     gain_lo = gain_ref[0:STRIDE, :]
     gain_hi = gain_ref[STRIDE:KERNEL, :]
     low = jnp.sum(keys3 * gain_lo[None], axis=1)
     high = jnp.sum(keys3 * gain_hi[None], axis=1)
     pool_v[me] = (low + jnp.concatenate([high[1:], high[:1]], axis=0)).astype(bf16)
-    part_v[me] = jnp.concatenate(
-        [jnp.broadcast_to(low[nb - 1 : nb], (8, DH)), jnp.broadcast_to(high[0:1], (8, DH))], axis=0
-    )
-    part_v[n] = jnp.zeros((16, DH), f32)
+    part_v[me, 0:1] = low[nb - 1 : nb]
+    part_v[me, 1:2] = high[0:1]
+    part_v[n] = jnp.zeros((8, DH), f32)
 
     @pl.when(me == n - 1)
     def _():
@@ -92,7 +99,8 @@
         return remote(pool_v.at[slot], pool_v.at[slot], pool_s.at[dst], pool_r.at[slot], dst)
 
     def part_copy(dst, slot):
-        return remote(part_v.at[slot], part_v.at[slot], part_s.at[dst], part_r.at[slot], dst)
+        pair = part_v.at[slot, pl.ds(0, 2)]
+        return remote(pair, pair, part_s.at[dst], part_r.at[slot], dst)
 
     def send_pool(k, _):
         dst = lax.rem(me + k, n)
@@ -118,19 +126,14 @@
         return 0
 
     lax.fori_loop(1, n, take_pool, 0)
-    last_row = lax.broadcasted_iota(jnp.int32, (nb, DH), 0) == nb - 1
-
-    def place_pool(d, _):
-        edge = part_v[d][0:1] + part_v[d + 1][8:9]
-        block = jnp.where(last_row, edge, pool_v[d].astype(f32)).astype(bf16)
-        at = pl.multiple_of(d * nb, nb)
-        pooled_v[pl.ds(at, nb), :] = block
-        comp_v[pl.ds(at, nb), :] = jnp.dot(
-            block, w_ref[...], preferred_element_type=f32
-        ).astype(bf16)
-        return 0
-
-    lax.fori_loop(0, n, place_pool, 0)
+    last_row = lax.broadcasted_iota(jnp.int32, (n, nb, DH), 1) == nb - 1
+    edges = part_v[0:n, 0:1, :] + part_v[1 : n + 1, 1:2, :]
+    pooled = jnp.where(last_row, edges, pool_v[...].astype(f32)).astype(bf16)
+    pooled_v[...] = pooled.reshape(count, DH)
+    w_copy.wait()
+    comp_v[...] = jnp.dot(
+        pooled_v[...], w_ref[...], preferred_element_type=f32
+    ).astype(bf16)
     q_copy.wait()
     t_copy.wait()
 
@@ -296,7 +299,10 @@
         a_out[d] = jnp.concatenate(pieces, axis=0)
 
     def a_copy(dst, slot):
-        return remote(a_out.at[dst], a_in.at[slot], a_s.at[dst], a_r.at[slot], dst)
+        used = pl.ds(0, rc + rg + 1)
+        return remote(
+            a_out.at[dst, used], a_in.at[slot, used], a_s.at[dst], a_r.at[slot], dst
+        )
 
     def send_a(k, _):
         a_copy(lax.rem(me + k, n), me).start()
@@ -317,7 +323,10 @@
     b_out[...] = lax.fori_loop(1, n, lambda d, total: total + a_in[d], a_in[0])
 
     def b_copy(dst, slot):
-        return remote(b_out, b_in.at[slot], b_s.at[dst], b_r.at[slot], dst)
+        used = pl.ds(0, rc + rg)
+        return remote(
+            b_out.at[used], b_in.at[slot, used], b_s.at[dst], b_r.at[slot], dst
+        )
 
     def send_b(k, _):
         b_copy(lax.rem(me + k, n), me).start()
@@ -361,6 +370,18 @@
         if (d + 1) * rg <= KERNEL:
             ggain_ref[d * rg : (d + 1) * rg, :] = b_in[d, rc : rc + rg, :]
     gq_copy.wait()
+
+
+def finish(*refs):
+    sources, targets, sem = refs[:5], refs[5:10], refs[10]
+    copies = [
+        pltpu.make_async_copy(source, target, sem.at[i])
+        for i, (source, target) in enumerate(zip(sources, targets))
+    ]
+    for copy in copies:
+        copy.start()
+    for copy in copies:
+        copy.wait()
 
 
 def body(n, keys, queries, teacher_map, slab_index, pos_gain, w_comp):
@@ -373,24 +394,28 @@
     slot_rows = -(-(rc + rg + 1) // 8) * 8
     dma = pltpu.SemaphoreType.DMA
     vmem = pl.BlockSpec(memory_space=pltpu.VMEM)
-    hbm = pl.BlockSpec(memory_space=pl.ANY)
-    loss, gq, gk, gcomp, ggain = pl.pallas_call(
-        functools.partial(kernel, n, rb, tr, rc, rg),
-        out_shape=(
+    hbm = pl.BlockSpec(memory_space=pltpu.HBM)
+    shapes = (
             jax.ShapeDtypeStruct((1, DH), f32),
             jax.ShapeDtypeStruct((rows, HEADS * DH), bf16),
             jax.ShapeDtypeStruct(keys.shape, bf16),
             jax.ShapeDtypeStruct((DH, DH), f32),
             jax.ShapeDtypeStruct((KERNEL, DH), f32),
-        ),
-        in_specs=[pl.BlockSpec(memory_space=pltpu.SMEM), vmem, vmem, vmem, hbm, hbm],
+        )
+    results = pl.pallas_call(
+        functools.partial(kernel, n, rb, tr, rc, rg),
+        out_shape=shapes,
+        in_specs=[pl.BlockSpec(memory_space=pltpu.SMEM)] + [hbm] * 5,
         out_specs=(vmem, hbm, vmem, vmem, vmem),
         scratch_shapes=[
+            pltpu.VMEM(keys.shape, bf16),
+            pltpu.VMEM(pos_gain.shape, f32),
+            pltpu.VMEM(w_comp.shape, bf16),
             pltpu.VMEM((rows, HEADS * DH), bf16),
             pltpu.VMEM((rows, count), bf16),
             pltpu.VMEM((rows, HEADS * DH), bf16),
             pltpu.VMEM((n, nb, DH), bf16),
-            pltpu.VMEM((n + 1, 16, DH), f32),
+            pltpu.VMEM((n + 1, 8, DH), f32),
             pltpu.VMEM((STRIDE, DH), bf16),
             pltpu.VMEM((count, DH), bf16),
             pltpu.VMEM((count, DH), bf16),
@@ -404,14 +429,23 @@
             pltpu.VMEM((n, slot_rows, DH), f32),
             pltpu.VMEM((nb, DH), f32),
             pltpu.VMEM((8, DH), f32),
-            dma((3,)),
+            dma((6,)),
         ]
         + [dma((n,))] * 10
         + [dma((4,))],
         compiler_params=pltpu.CompilerParams(
             collective_id=0, has_side_effects=True, vmem_limit_bytes=48 * 1024 * 1024
         ),
-    )(slab_index, keys, pos_gain, w_comp, queries, teacher_map)
+    )(slab_index, *[pltpu.with_memory_space_constraint(x, pltpu.HBM) for x in (keys, pos_gain, w_comp, queries, teacher_map)])
+    any_space = pl.BlockSpec(memory_space=pl.ANY)
+    loss, gq, gk, gcomp, ggain = pl.pallas_call(
+        finish,
+        out_shape=shapes,
+        in_specs=[any_space] * 5,
+        out_specs=[any_space] * 5,
+        scratch_shapes=[dma((5,))],
+        compiler_params=pltpu.CompilerParams(vmem_limit_bytes=4 * 1024 * 1024),
+    )(*results)
     return (loss[0, 0:1], gq, gk, gcomp, ggain)
 
 

time: 49.1 us -> 36.9 us (0.75)
  local copies, waits for them, and re-layouts: 7.05 us -> 0 us
  Pallas kernels: 39.2 us -> 35.4 us
  between operations: 2.46 us -> 1.29 us
    unnamed x14 -> x0, local copies, waits for them, and re-layouts: 7.05 us -> none
    pallas_call x1 -> x2, Pallas kernels: 39.2 us -> 35.4 us  [the longest x1 34.5 us: body(): pl.pallas_call(functools.partial(kernel, n, rb, tr, rc, rg), out_shape=sh...]
where the time goes in v2:
time: 36.9 us; the launch traced here: 36.7 us
  Pallas kernels  35.4 us (96%)
  between operations  1.29 us (3%)
    pallas_call x1, Pallas kernels, body(): pl.pallas_call(functools.partial(kernel, n, rb, tr, rc, rg), out_shape=sh...  34.5 us
    pallas_call x1, Pallas kernels, body(): pl.pallas_call(finish, out_shape=shapes, in_specs=[any_space] * 5, out_sp...  0.9 us

profile of v2, /device:TPU:0, one launch (start us, length us, event | category | flops | bytes accessed | tf_op | source)
XLA Modules:
  0.0 36.7 jit_solution(1896756466632472048)
XLA Ops:
  1.3 34.5 %shard_map.101 = (f32[1,128]{1,0:T(1,128)S(1)}, bf16[256,1024]{1,0:T(8,128)(2,1)S(1)}, bf16[512,128]{1,0:T(8,128)(2,1)S(1)}, f32[128,128]{1,0:T(8,128)S(1)}, f32[32,128]{1,0:T(8,128)S(1)}) custom-call(s32[1]{0:T(128)S(6)} %copy.11.slab_ref, bf16[512,128]{1,0:T(8,128)(2,1)} %keys_hbm.1, f32[32,128]{1,0:T(8,128)} %gain_hbm.1, bf16[128,128]{1,0:T(8,128)(2,1)} %w_hbm.1, ...), custom_call_target="tpu_custom_call" | custom-call | tf_op jit(solution)/shard_map/pallas_call | solution.py:405
  35.8 0.9 %shard_map.102 = (f32[1,128]{1,0:T(1,128)}, bf16[256,1024]{1,0:T(8,128)(2,1)}, bf16[512,128]{1,0:T(8,128)(2,1)}, f32[128,128]{1,0:T(8,128)}, f32[32,128]{1,0:T(8,128)}) custom-call(f32[1,128]{1,0:T(1,128)S(1)} %get-tuple-element.15.refs_0_, bf16[256,1024]{1,0:T(8,128)(2,1)S(1)} %get-tuple-element.16.refs_1_, bf16[512,128]{1,0:T(8,128)(2,1)S(1)} %get-tuple-element.17.refs_2_, ...), custom_call_target="tpu_custom_call" | custom-call | tf_op jit(solution)/shard_map/pallas_call | solution.py:441

commit v3 on v2

--- a/solution.py
+++ b/solution.py
@@ -42,14 +42,25 @@
     n, rb, tr, rc, rg,
     slab_ref, keys_hbm, gain_hbm, w_hbm, q_hbm, t_hbm,
     loss_ref, gq_hbm, gk_ref, gcomp_ref, ggain_ref,
-    keys_ref, gain_ref, w_ref, q_v, t_v, gq_v, pool_v, part_v, halo_v, pooled_v, comp_v, s_v, g_v, p_v, rs_v,
+    keys_ref, gain_ref, w_ref, q_v, t_v, gq_v, pool_v, part_v, halo_v, pooled_v, comp_v, s_v, g_v, p_v, pair_v, rs_v,
     a_out, a_in, b_out, b_in, gp_v, carry_v,
-    local_sem, pool_s, pool_r, part_s, part_r, rs_s, rs_r, a_s, a_r, b_s, b_r, side_sem,
+    local_sem, pool_s, pool_r, part_s, part_r, pair_s, pair_r, rs_s, rs_r, a_s, a_r, b_s, b_r, side_sem,
 ):
     me = lax.axis_index("ctx")
     rows, count = t_v.shape
     nb = count // n
     inv = DH ** (-0.5)
+
+    barrier = pltpu.get_barrier_semaphore()
+
+    def greet(k, _):
+        pl.semaphore_signal(
+            barrier, inc=1, device_id={"ctx": lax.rem(me + k, n)},
+            device_id_type=pl.DeviceIdType.MESH,
+        )
+        return 0
+
+    lax.fori_loop(1, n, greet, 0)
 
     q_copy = pltpu.make_async_copy(q_hbm, q_v, local_sem.at[0])
     t_copy = pltpu.make_async_copy(t_hbm, t_v, local_sem.at[1])
@@ -61,17 +72,6 @@
     w_copy.start()
     q_copy.start()
     t_copy.start()
-
-    barrier = pltpu.get_barrier_semaphore()
-
-    def greet(k, _):
-        pl.semaphore_signal(
-            barrier, inc=1, device_id={"ctx": lax.rem(me + k, n)},
-            device_id_type=pl.DeviceIdType.MESH,
-        )
-        return 0
-
-    lax.fori_loop(1, n, greet, 0)
 
     keys_copy.wait()
     gain_copy.wait()
@@ -200,10 +200,13 @@
                     preferred_element_type=f32,
                 )
             add = acc.T * inv
-            if first is None:
-                p_v[c0 : c0 + CHUNK, :] = add
-            else:
-                p_v[c0 : c0 + CHUNK, :] = p_v[c0 : c0 + CHUNK, :] + add
+            for r0 in range(0, CHUNK, nb):
+                owner = (c0 + r0) // nb
+                at = (owner % 2, owner // 2)
+                if first is None:
+                    p_v[at] = add[r0 : r0 + nb]
+                else:
+                    p_v[at] = p_v[at] + add[r0 : r0 + nb]
         return kl
 
     def query_grads(base):
@@ -226,16 +229,37 @@
 
         kl = lax.fori_loop(0, rows // rb, step, kl0)
 
+    core = lax.rem(me, 2)
+    mine = lax.div(me, 2)
+    half = n // 2
+    twin = me + 1 - 2 * core
+
+    def pair_copy(slot):
+        return remote(
+            p_v.at[1 - core, slot], pair_v.at[slot], pair_s.at[slot], pair_r.at[slot], twin
+        )
+
     def rs_copy(dst, slot):
-        at = pl.multiple_of(dst * nb, nb)
-        return remote(p_v.at[pl.ds(at, nb)], rs_v.at[slot], rs_s.at[dst], rs_r.at[slot], dst)
-
-    def send_rs(k, _):
-        rs_copy(lax.rem(me + k, n), me).start()
-        return 0
-
-    lax.fori_loop(1, n, send_rs, 0)
-    rs_v[me] = p_v[pl.ds(pl.multiple_of(me * nb, nb), nb), :]
+        return remote(
+            p_v.at[core, dst], rs_v.at[slot], rs_s.at[dst], rs_r.at[slot], 2 * dst + core
+        )
+
+    def send_pair(k, _):
+        pair_copy(lax.rem(mine + k, half)).start()
+        return 0
+
+    lax.fori_loop(1, half + 1, send_pair, 0)
+
+    def forward(k, _):
+        slot = lax.rem(mine + k, half)
+        pair_copy(slot).wait_recv()
+        p_v[core, slot] = p_v[core, slot] + pair_v[slot]
+        rs_copy(slot, mine).start()
+        return 0
+
+    lax.fori_loop(1, half, forward, 0)
+    pair_copy(mine).wait_recv()
+    rs_v[mine] = p_v[core, mine] + pair_v[mine]
 
     if rb == rows:
         query_grads(0)
@@ -251,11 +275,12 @@
     )
 
     def take_rs(k, _):
-        rs_copy(lax.rem(me + k, n), lax.rem(me + k, n)).wait_recv()
-        return 0
-
-    lax.fori_loop(1, n, take_rs, 0)
-    own = lax.fori_loop(1, n, lambda d, total: total + rs_v[d], rs_v[0])
+        slot = lax.rem(mine + k, half)
+        rs_copy(slot, slot).wait_recv()
+        return 0
+
+    lax.fori_loop(1, half, take_rs, 0)
+    own = lax.fori_loop(1, half, lambda d, total: total + rs_v[d], rs_v[0])
 
     own3 = split3(own)
     gp3 = lax.dot_general(
@@ -344,11 +369,19 @@
         dst = lax.rem(me + k, n)
         pool_copy(dst, me).wait_send()
         part_copy(dst, me).wait_send()
-        rs_copy(dst, me).wait_send()
         a_copy(dst, me).wait_send()
         return 0
 
     lax.fori_loop(1, n, drop_sends, 0)
+
+    def drop_pairs(k, _):
+        slot = lax.rem(mine + k, half)
+        pair_copy(slot).wait_send()
+        rs_copy(slot, mine).wait_send()
+        return 0
+
+    lax.fori_loop(1, half, drop_pairs, 0)
+    pair_copy(mine).wait_send()
 
     @pl.when(me > 0)
     def _():
@@ -388,7 +421,7 @@
     rows, count = teacher_map.shape
     nb = count // n
     rb = rows if count <= 1024 else 32
-    tr = min(rb, 32 if count <= 1024 else 16)
+    tr = min(rb, 64 if count <= 1024 else 16)
     rc = -(-DH // n)
     rg = -(-KERNEL // n)
     slot_rows = -(-(rc + rg + 1) // 8) * 8
@@ -421,8 +454,9 @@
             pltpu.VMEM((count, DH), bf16),
             pltpu.VMEM((HEADS, rb, count), f32),
             pltpu.VMEM((HEADS, rb, count), bf16),
-            pltpu.VMEM((count, DH), f32),
-            pltpu.VMEM((n, nb, DH), f32),
+            pltpu.VMEM((2, n // 2, nb, DH), f32),
+            pltpu.VMEM((n // 2, nb, DH), f32),
+            pltpu.VMEM((n // 2, nb, DH), f32),
             pltpu.VMEM((n, slot_rows, DH), f32),
             pltpu.VMEM((n, slot_rows, DH), f32),
             pltpu.VMEM((slot_rows, DH), f32),
@@ -431,7 +465,9 @@
             pltpu.VMEM((8, DH), f32),
             dma((6,)),
         ]
-        + [dma((n,))] * 10
+        + [dma((n,))] * 4
+        + [dma((n // 2,))] * 4
+        + [dma((n,))] * 4
         + [dma((4,))],
         compiler_params=pltpu.CompilerParams(
             collective_id=0, has_side_effects=True, vmem_limit_bytes=48 * 1024 * 1024

time: 36.9 us -> 35 us (0.949)
  Pallas kernels: 35.4 us -> 33.6 us
    pallas_call x1, Pallas kernels: 34.5 us -> 32.7 us  [body(): pl.pallas_call(functools.partial(kernel, n, rb, tr, rc, rg), out_shape=sh...]
where the time goes in v3:
time: 35 us; the launch traced here: 34.9 us
  Pallas kernels  33.6 us (96%)
  between operations  1.29 us (4%)
    pallas_call x1, Pallas kernels, body(): pl.pallas_call(functools.partial(kernel, n, rb, tr, rc, rg), out_shape=sh...  32.7 us
    pallas_call x1, Pallas kernels, body(): pl.pallas_call(finish, out_shape=shapes, in_specs=[any_space] * 5, out_sp...  0.9 us

profile of v3, /device:TPU:0, one launch (start us, length us, event | category | flops | bytes accessed | tf_op | source)
XLA Modules:
  0.0 34.9 jit_solution(15756855132590918733)
XLA Ops:
  1.3 32.7 %shard_map.101 = (f32[1,128]{1,0:T(1,128)S(1)}, bf16[256,1024]{1,0:T(8,128)(2,1)S(1)}, bf16[512,128]{1,0:T(8,128)(2,1)S(1)}, f32[128,128]{1,0:T(8,128)S(1)}, f32[32,128]{1,0:T(8,128)S(1)}) custom-call(s32[1]{0:T(128)S(6)} %copy.11.slab_ref, bf16[512,128]{1,0:T(8,128)(2,1)} %keys_hbm.1, f32[32,128]{1,0:T(8,128)} %gain_hbm.1, bf16[128,128]{1,0:T(8,128)(2,1)} %w_hbm.1, ...), custom_call_target="tpu_custom_call" | custom-call | tf_op jit(solution)/shard_map/pallas_call | solution.py:438
  34.0 0.9 %shard_map.102 = (f32[1,128]{1,0:T(1,128)}, bf16[256,1024]{1,0:T(8,128)(2,1)}, bf16[512,128]{1,0:T(8,128)(2,1)}, f32[128,128]{1,0:T(8,128)}, f32[32,128]{1,0:T(8,128)}) custom-call(f32[1,128]{1,0:T(1,128)S(1)} %get-tuple-element.15.refs_0_, bf16[256,1024]{1,0:T(8,128)(2,1)S(1)} %get-tuple-element.16.refs_1_, bf16[512,128]{1,0:T(8,128)(2,1)S(1)} %get-tuple-element.17.refs_2_, ...), custom_call_target="tpu_custom_call" | custom-call | tf_op jit(solution)/shard_map/pallas_call | solution.py:477

commit v4 on v3

--- a/solution.py
+++ b/solution.py
@@ -11,7 +11,7 @@
 HEADS = 8
 KERNEL = 32
 STRIDE = 16
-CHUNK = 512
+CHUNK = 256
 
 big_negative = -1e30
 loss_scale = 256.0
@@ -41,8 +41,8 @@
 def kernel(
     n, rb, tr, rc, rg,
     slab_ref, keys_hbm, gain_hbm, w_hbm, q_hbm, t_hbm,
-    loss_ref, gq_hbm, gk_ref, gcomp_ref, ggain_ref,
-    keys_ref, gain_ref, w_ref, q_v, t_v, gq_v, pool_v, part_v, halo_v, pooled_v, comp_v, s_v, g_v, p_v, pair_v, rs_v,
+    loss_ref, gq_ref, gk_ref, gcomp_ref, ggain_ref,
+    keys_ref, gain_ref, w_ref, q_v, t_v, pool_v, part_v, halo_v, pooled_v, comp_v, s_v, g_v, p_v, pair_v, rs_v,
     a_out, a_in, b_out, b_in, gp_v, carry_v,
     local_sem, pool_s, pool_r, part_s, part_r, pair_s, pair_r, rs_s, rs_r, a_s, a_r, b_s, b_r, side_sem,
 ):
@@ -211,7 +211,7 @@
 
     def query_grads(base):
         for h in range(HEADS):
-            gq_v[pl.ds(base, rb), h * DH : (h + 1) * DH] = (
+            gq_ref[pl.ds(base, rb), h * DH : (h + 1) * DH] = (
                 jnp.dot(g_v[h], comp_v[...], preferred_element_type=f32) * inv
             ).astype(bf16)
 
@@ -263,8 +263,6 @@
 
     if rb == rows:
         query_grads(0)
-    gq_copy = pltpu.make_async_copy(gq_v, gq_hbm, local_sem.at[2])
-    gq_copy.start()
 
     @pl.when(me < n - 1)
     def _():
@@ -402,7 +400,6 @@
         gcomp_ref[d * rc : (d + 1) * rc, :] = b_in[d, 0:rc, :]
         if (d + 1) * rg <= KERNEL:
             ggain_ref[d * rg : (d + 1) * rg, :] = b_in[d, rc : rc + rg, :]
-    gq_copy.wait()
 
 
 def finish(*refs):
@@ -439,14 +436,13 @@
         functools.partial(kernel, n, rb, tr, rc, rg),
         out_shape=shapes,
         in_specs=[pl.BlockSpec(memory_space=pltpu.SMEM)] + [hbm] * 5,
-        out_specs=(vmem, hbm, vmem, vmem, vmem),
+        out_specs=(vmem,) * 5,
         scratch_shapes=[
             pltpu.VMEM(keys.shape, bf16),
             pltpu.VMEM(pos_gain.shape, f32),
             pltpu.VMEM(w_comp.shape, bf16),
             pltpu.VMEM((rows, HEADS * DH), bf16),
             pltpu.VMEM((rows, count), bf16),
-            pltpu.VMEM((rows, HEADS * DH), bf16),
             pltpu.VMEM((n, nb, DH), bf16),
             pltpu.VMEM((n + 1, 8, DH), f32),
             pltpu.VMEM((STRIDE, DH), bf16),

time: 35 us -> 34.8 us (level)
  no operation moved by 1% of the time
where the time goes in v4:
time: 34.8 us; the launch traced here: 34.7 us
  Pallas kernels  33.4 us (96%)
  between operations  1.29 us (4%)
    pallas_call x1, Pallas kernels, body(): pl.pallas_call(functools.partial(kernel, n, rb, tr, rc, rg), out_shape=sh...  32.5 us
    pallas_call x1, Pallas kernels, body(): pl.pallas_call(finish, out_shape=shapes, in_specs=[any_space] * 5, out_sp...  0.9 us

profile of v4, /device:TPU:0, one launch (start us, length us, event | category | flops | bytes accessed | tf_op | source)
XLA Modules:
  0.0 34.7 jit_solution(14986808693174898741)
XLA Ops:
  1.3 32.5 %shard_map.101 = (f32[1,128]{1,0:T(1,128)S(1)}, bf16[256,1024]{1,0:T(8,128)(2,1)S(1)}, bf16[512,128]{1,0:T(8,128)(2,1)S(1)}, f32[128,128]{1,0:T(8,128)S(1)}, f32[32,128]{1,0:T(8,128)S(1)}) custom-call(s32[1]{0:T(128)S(6)} %copy.11.slab_ref, bf16[512,128]{1,0:T(8,128)(2,1)} %keys_hbm.1, f32[32,128]{1,0:T(8,128)} %gain_hbm.1, bf16[128,128]{1,0:T(8,128)(2,1)} %w_hbm.1, ...), custom_call_target="tpu_custom_call" | custom-call | tf_op jit(solution)/shard_map/pallas_call | solution.py:435
  33.8 0.9 %shard_map.102 = (f32[1,128]{1,0:T(1,128)}, bf16[256,1024]{1,0:T(8,128)(2,1)}, bf16[512,128]{1,0:T(8,128)(2,1)}, f32[128,128]{1,0:T(8,128)}, f32[32,128]{1,0:T(8,128)}) custom-call(f32[1,128]{1,0:T(1,128)S(1)} %get-tuple-element.15.refs_0_, bf16[256,1024]{1,0:T(8,128)(2,1)S(1)} %get-tuple-element.16.refs_1_, bf16[512,128]{1,0:T(8,128)(2,1)S(1)} %get-tuple-element.17.refs_2_, ...), custom_call_target="tpu_custom_call" | custom-call | tf_op jit(solution)/shard_map/pallas_call | solution.py:473
